TPU v7x, 32 devices: a whole 2x2x4 slice. The times are simulated.
32 devices in a mesh: sat: 8 (over z, x), tm: 4 (over y, core).
Axes of the slice: x: 2, y: 2, z: 4, core: 2. Of those that a mesh axis runs over, the one named last changes fastest.
Arguments:
- panels: bfloat16 [64, 32, 64, 128], P('sat', 'tm'), may hold values from -0.3125 to 0.3125
- weights: bfloat16 [64, 32, 64], P('sat', 'tm'), may hold values from 0.19921875 to 5
- pair_members: int32 [32, 2], P('sat'), may hold values from 0 to 63, as said below
- pair_live: int32 [32, 32], P('tm', 'sat'), may hold values 0 or 1
Outputs:
- normal_rows: float32 [12288, 128], P(('sat', 'tm'))
Inputs may be any that keep to these rules, and one draw needn't show every extreme that they name: `pair_members`: every satellite is a member of exactly one baseline, and both members of baseline p are satellites whose numbers leave the remainder p // 4 when divided by 8.
All inputs are finite; a program needn't handle non-finite values. No bound on the sum of `pair_live` on one device may be relied on, other than what follows from the above.
Results may differ from a plain program's by a relative error of at most 0.0009.
Values may be sent and summed in bfloat16 or wider, within the bound.
A program may use at most 64 MiB of HBM per device.

v0:
```python
import jax
import jax.numpy as jnp
from jax import lax
from jax.sharding import PartitionSpec as P


def scale_rows(root_weight, panel):
    scaled = (root_weight[..., None] * panel).astype(jnp.bfloat16)
    return scaled.reshape(panel.shape[0], -1, panel.shape[-1])


def per_device(panels, weights, pair_members, pair_live):
    sat_count = lax.axis_size("sat")
    params = panels.shape[-1]
    moved_panels, moved_weights = (
        lax.all_to_all(panels, "sat", split_axis=0, concat_axis=0, tiled=True),
        lax.all_to_all(weights, "sat", split_axis=0, concat_axis=0, tiled=True),
    )
    source_ids = pair_members // sat_count
    first_panel = moved_panels[source_ids[:, 0]]
    second_panel = moved_panels[source_ids[:, 1]]
    first_value = moved_weights[source_ids[:, 0]].astype(jnp.float32)
    second_value = moved_weights[source_ids[:, 1]].astype(jnp.float32)
    live_pair = jnp.transpose(pair_live).astype(jnp.float32)
    dd_weight = live_pair[:, :, None] * first_value * second_value / (first_value + second_value)
    root_weight = jnp.sqrt(dd_weight)
    first_scaled = scale_rows(root_weight, first_panel)
    second_scaled = scale_rows(root_weight, second_panel)
    first_gram = jnp.einsum(
        "pkx,pky->pxy", first_scaled, first_scaled, preferred_element_type=jnp.float32
    )
    cross_gram = -jnp.einsum(
        "pkx,pky->pxy", first_scaled, second_scaled, preferred_element_type=jnp.float32
    )
    second_gram = jnp.einsum(
        "pkx,pky->pxy", second_scaled, second_scaled, preferred_element_type=jnp.float32
    )
    stacked = jnp.stack([first_gram, cross_gram, second_gram], axis=1).reshape(-1, params)
    result_rows = lax.psum_scatter(stacked, "tm", scatter_dimension=0, tiled=True)
    return result_rows


def solution(mesh):
    in_specs = (P("sat", "tm", None, None), P("sat", "tm", None), P("sat", None), P("tm", "sat"))
    out_specs = P(("sat", "tm"), None)
    return jax.shard_map(
        per_device, mesh=mesh, in_specs=in_specs, out_specs=out_specs, check_vma=False
    )
```

profile of v0, /device:TPU:0, one launch (start us, length us, event | category | flops | bytes accessed | tf_op | source)
XLA Modules:
  0.0 82.6 jit_solution(3493411970672248540)
XLA Ops:
  6.5 0.8 reshape.72
  7.3 13.6 %all_to_all.10 = bf16[8,2,256]{2,1,0:T(2,128)(2,1)S(1)} all-to-all(bf16[8,2,256]{2,1,0:T(2,128)(2,1)S(1)} %reshape.72), channel_id=1, replica_groups=mesh['sat'=8,'tm'=4] {'sat'}, dimensions={0} | all-to-all | bytes 16384 | tf_op jit(solution)/shard_map/all_to_all | solution.py:17
  20.9 0.0 copy-start
  20.9 3.7 %all-to-all-start.1 = ((bf16[8,8,64,128]{3,2,1,0:T(8,128)(2,1)}), bf16[8,8,64,128]{3,2,1,0:T(8,128)(2,1)S(1)}, u32[]{:S(2)}, u32[]{:S(2)}) async-start(bf16[8,8,64,128]{3,2,1,0:T(8,128)(2,1)} %param.4), calls=%async_computation.1 | async-start | bytes 2097152 | tf_op jit(solution)/shard_map/all_to_all | solution.py:16
  24.6 0.0 reduce-scatter.2.cloned.1.call-start
  24.6 0.0 copy-done
  24.7 0.1 mul.37
  24.7 0.0 copy-start.1
  24.7 0.1 mul.38
  24.8 0.6 copy-done.1
  25.4 0.1 reshape.73
  25.5 0.6 gather_fusion
  26.1 0.1 reshape.36
  26.2 0.6 gather_fusion.1
  26.8 0.1 reshape.37
  26.9 22.5 %all-to-all-done.1 = bf16[8,8,64,128]{3,2,1,0:T(8,128)(2,1)S(1)} async-done(((bf16[8,8,64,128]{3,2,1,0:T(8,128)(2,1)}), bf16[8,8,64,128]{3,2,1,0:T(8,128)(2,1)S(1)}, u32[]{:S(2)}, u32[]{:S(2)}) %all-to-all-start.1) | async-done | bytes 1048608 | tf_op jit(solution)/shard_map/all_to_all | solution.py:16
  49.3 0.6 gather_fusion.2
  50.0 0.1 bitcast_convert_fusion.1
  50.1 0.3 copy.10
  50.4 0.6 gather_fusion.3
  51.1 0.1 bitcast_convert_fusion
  51.2 0.3 copy.12
  51.5 0.3 convolution_bitcast_fusion.1
  51.9 0.3 fusion
  52.2 0.3 convolution_bitcast_fusion
  52.5 0.1 pad_maximum_fusion
  52.5 0.9 %copy.15 = f32[4,3,128,128]{3,2,1,0:T(8,128)} copy(f32[4,3,128,128]{3,2,0,1:T(8,128)S(1)} %pad_maximum_fusion) | data formatting | bytes 1572864 | tf_op jit(solution)/shard_map/stack | solution.py:38
  53.5 0.0 reduce-scatter.2.cloned.1.call-update
  53.5 22.3 %reduce-scatter.2.cloned.1.call-done = f32[384,128]{1,0:T(8,128)} async-done(((f32[1536,128]{1,0:T(8,128)}), f32[384,128]{1,0:T(8,128)}) %reduce-scatter.2.cloned.1.call-update) | async-done | bytes 196624 | tf_op jit(solution)/shard_map/reduce_scatter | solution.py:39
  (5 shorter events, 0.0 us)
Async XLA Ops:
  20.9 3.8 %copy-start = (s32[8,4]{0,1:T(4,128)S(1)}, s32[8,4]{0,1:T(4,128)}, u32[]{:S(2)}) copy-start(s32[8,4]{0,1:T(4,128)} %param.7) | copy-start | bytes 388
  20.9 28.4 %all-to-all-start.1 = ((bf16[8,8,64,128]{3,2,1,0:T(8,128)(2,1)}), bf16[8,8,64,128]{3,2,1,0:T(8,128)(2,1)S(1)}, u32[]{:S(2)}, u32[]{:S(2)}) async-start(bf16[8,8,64,128]{3,2,1,0:T(8,128)(2,1)} %param.4), calls=%async_computation.1 | async-start | bytes 2097152 | tf_op jit(solution)/shard_map/all_to_all | solution.py:16
  24.6 51.2 %reduce-scatter.2.cloned.1.call-start = ((), (), s32[]{:S(2)}) async-start(), calls=%async_computation.3 | async-start | bytes 983040 | tf_op jit(solution)/shard_map/reduce_scatter | solution.py:39
  24.7 0.7 copy-start.1
Sparse Core Ops, SparseCore 0:
  53.6 22.1 reduce-scatter.1
where the time goes:
time: 83 us; the launch traced here: 82.6 us
  waiting for transfers between devices  44.8 us (54%)
  blocking collectives  13.6 us (16%)
  between operations  13.5 us (16%)
  local copies, waits for them, and re-layouts  5.86 us (7%)
  starting transfers between devices  3.73 us (4%)
  matrix products  0.92 us (1%)
    all_to_all x1, waiting for transfers between devices, per_device(): lax.all_to_all(panels, 'sat', split_axis=0, concat_axis=0, tiled=True)  22.5 us
    reduce_scatter x1, waiting for transfers between devices, per_device(): lax.psum_scatter(stacked, 'tm', scatter_dimension=0, tiled=True)  22.3 us
    all_to_all x1, blocking collectives, per_device(): lax.all_to_all(weights, 'sat', split_axis=0, concat_axis=0, tiled=True)  13.6 us
    all_to_all x1, starting transfers between devices, per_device(): lax.all_to_all(panels, 'sat', split_axis=0, concat_axis=0, tiled=True)  3.69 us
  transfers between devices with their start and end apart: 2, of which 2 were waited for; matrix products, arithmetic and copies ran while one was open for 2% of the time, Pallas kernels for 0%

commit v1 on v0

v1 whole, which is shorter than its diff:
```python
import functools
import jax
import jax.numpy as jnp
from jax import lax
from jax.experimental import pallas as pl
from jax.experimental.pallas import tpu as pltpu
from jax.sharding import PartitionSpec as P

MESH = pl.DeviceIdType.MESH
CHUNKS = 4


def kernel(nsat, ntm, panels, weights, members, live_ref, out_ref, *scratch):
    held = scratch[:CHUNKS]
    (heldw, root_ref, scaled, acc, gram, arrived,
     psend, precv, wsend, wrecv, gsend, grecv) = scratch[CHUNKS:]
    epochs, rows, params = panels.shape[1:]
    pairs = members.shape[0]
    per_owner = pairs // ntm
    step = epochs // CHUNKS
    s = lax.axis_index("sat")
    t = lax.axis_index("tm")

    barrier = pltpu.get_barrier_semaphore()

    def greet(axis, me, n):
        def body(k, carry):
            pl.semaphore_signal(barrier, inc=1, device_id={axis: lax.rem(me + k, n)}, device_id_type=MESH)
            return carry
        lax.fori_loop(1, n, body, 0)

    greet("sat", s, nsat)
    greet("tm", t, ntm)

    def weight_copy(k):
        dest = lax.rem(s + k, nsat)
        return pltpu.make_async_remote_copy(
            src_ref=weights.at[dest], dst_ref=heldw.at[s],
            send_sem=wsend.at[k], recv_sem=wrecv.at[k],
            device_id={"sat": dest}, device_id_type=MESH)

    def weight_arrival(k):
        source = lax.rem(s + nsat - k, nsat)
        return pltpu.make_async_remote_copy(
            src_ref=weights.at[s], dst_ref=heldw.at[source],
            send_sem=wsend.at[k], recv_sem=wrecv.at[k],
            device_id={"sat": source}, device_id_type=MESH)

    def panel_copy(c, k):
        dest = lax.rem(s + k, nsat)
        part = pl.ds(c * step, step)
        return pltpu.make_async_remote_copy(
            src_ref=panels.at[dest, part], dst_ref=held[c].at[s],
            send_sem=psend.at[c, k], recv_sem=precv.at[c, k],
            device_id={"sat": dest}, device_id_type=MESH)

    def panel_arrival(c, k):
        source = lax.rem(s + nsat - k, nsat)
        part = pl.ds(c * step, step)
        return pltpu.make_async_remote_copy(
            src_ref=panels.at[s, part], dst_ref=held[c].at[source],
            send_sem=psend.at[c, k], recv_sem=precv.at[c, k],
            device_id={"sat": source}, device_id_type=MESH)

    own_panels = [
        pltpu.make_async_copy(panels.at[s, pl.ds(c * step, step)], held[c].at[s], psend.at[c, 0])
        for c in range(CHUNKS)
    ]
    own_weight = pltpu.make_async_copy(weights.at[s], heldw.at[s], wsend.at[0])
    for copy in own_panels:
        copy.start()
    own_weight.start()

    pl.semaphore_wait(barrier, nsat - 1 + ntm - 1)

    def each(n, f):
        def body(k, carry):
            f(k)
            return carry
        lax.fori_loop(1, n, body, 0)

    each(nsat, lambda k: weight_copy(k).start())
    for c in range(CHUNKS):
        each(nsat, lambda k: panel_copy(c, k).start())

    root_ref[...] = jnp.zeros_like(root_ref)
    live_all = live_ref[...].astype(jnp.float32)
    pair_lane = lax.broadcasted_iota(jnp.int32, live_all.shape, 1)
    offsets = [ntm // 2] + [k for k in range(ntm - 1, 0, -1) if k != ntm // 2] + [0]
    slots = [(k, r) for k in offsets for r in range(per_owner)]
    owners = {k: lax.rem(t + k, ntm) for k in offsets}

    own_weight.wait()
    each(nsat, lambda k: weight_arrival(k).wait_recv())
    firsts, seconds = [], []
    for n, (k, r) in enumerate(slots):
        pair = owners[k] * per_owner + r
        first, second = members[pair, 0] // nsat, members[pair, 1] // nsat
        firsts.append(first)
        seconds.append(second)
        u = heldw[first].astype(jnp.float32)
        v = heldw[second].astype(jnp.float32)
        live = jnp.sum(jnp.where(pair_lane == pair, live_all, 0.0), axis=1, keepdims=True)
        root_ref[n * epochs:(n + 1) * epochs, :rows] = jnp.sqrt(live * u * v / (u + v))
    root = jnp.transpose(root_ref[...])

    def gram_copy(k):
        return pltpu.make_async_remote_copy(
            src_ref=gram.at[k], dst_ref=arrived.at[k],
            send_sem=gsend.at[k], recv_sem=grecv.at[k],
            device_id={"tm": lax.rem(t + k, ntm)}, device_id_type=MESH)

    for c in range(CHUNKS):
        own_panels[c].wait()
        each(nsat, lambda k: panel_arrival(c, k).wait_recv())
        for n, (k, r) in enumerate(slots):
            for e in range(step):
                at = c * step + e
                column = root[:rows, n * epochs + at:n * epochs + at + 1]
                here = slice(e * rows, (e + 1) * rows)
                scaled[n % 2, here, :params] = (column * held[c][firsts[n], e].astype(jnp.float32)).astype(jnp.bfloat16)
                scaled[n % 2, here, params:] = (column * held[c][seconds[n], e].astype(jnp.float32)).astype(jnp.bfloat16)
            both = scaled[n % 2]
            product = lax.dot_general(both, both, (((0,), (0,)), ((), ())), preferred_element_type=jnp.float32)
            if c > 0:
                product = product + acc[n]
            if c < CHUNKS - 1:
                acc[n] = product
                continue
            base = r * 3 * params
            gram[k, base:base + params] = product[:params, :params]
            gram[k, base + params:base + 2 * params] = -product[:params, params:]
            gram[k, base + 2 * params:base + 3 * params] = product[params:, params:]
            if k > 0 and r == per_owner - 1:
                gram_copy(k).start()

    total = gram[0]
    for k in offsets[:-1]:
        gram_copy(k).wait_recv()
        total = total + arrived[k]
    out_ref[...] = total

    each(nsat, lambda k: weight_copy(k).wait_send())
    for c in range(CHUNKS):
        each(nsat, lambda k: panel_copy(c, k).wait_send())
    for k in offsets[:-1]:
        gram_copy(k).wait_send()


def per_device(panels, weights, pair_members, pair_live):
    nsat, ntm = lax.axis_size("sat"), lax.axis_size("tm")
    sats, epochs, rows, params = panels.shape
    pairs = pair_members.shape[0]
    out_rows = pairs // ntm * 3 * params
    root_rows = -(-pairs * epochs // 128) * 128
    dma = pltpu.SemaphoreType.DMA
    vmem = pl.BlockSpec(memory_space=pltpu.VMEM)
    hbm = pl.BlockSpec(memory_space=pl.ANY)
    return pl.pallas_call(
        functools.partial(kernel, nsat, ntm),
        out_shape=jax.ShapeDtypeStruct((out_rows, params), jnp.float32),
        in_specs=[hbm, hbm, pl.BlockSpec(memory_space=pltpu.SMEM), vmem],
        out_specs=vmem,
        scratch_shapes=[
            *[pltpu.VMEM((nsat, epochs // CHUNKS, rows, params), jnp.bfloat16)] * CHUNKS,
            pltpu.VMEM((nsat, epochs, rows), jnp.bfloat16),
            pltpu.VMEM((root_rows, 128), jnp.float32),
            pltpu.VMEM((2, epochs // CHUNKS * rows, 2 * params), jnp.bfloat16),
            pltpu.VMEM((pairs, 2 * params, 2 * params), jnp.float32),
            pltpu.VMEM((ntm, out_rows, params), jnp.float32),
            pltpu.VMEM((ntm, out_rows, params), jnp.float32),
            dma((CHUNKS, nsat)), dma((CHUNKS, nsat)),
            dma((nsat,)), dma((nsat,)),
            dma((ntm,)), dma((ntm,)),
        ],
        compiler_params=pltpu.CompilerParams(
            collective_id=0, has_side_effects=True, vmem_limit_bytes=48 << 20),
    )(panels, weights, pair_members, pair_live)


def solution(mesh):
    in_specs = (P("sat", "tm", None, None), P("sat", "tm", None), P("sat", None), P("tm", "sat"))
    out_specs = P(("sat", "tm"), None)
    return jax.shard_map(
        per_device, mesh=mesh, in_specs=in_specs, out_specs=out_specs, check_vma=False
    )
```

time: 83 us -> 43.8 us (0.53)
  the two profiles are of different devices: /device:TPU:0 before, /device:TPU:11 now
where the time goes in v1:
time: 43.8 us; the launch traced here: 43.5 us
  Pallas kernels  40.1 us (92%)
  local copies, waits for them, and re-layouts  3.48 us (8%)
    pallas_call x1, Pallas kernels, per_device(): pl.pallas_call(functools.partial(kernel, nsat, ntm), out_shape=jax.ShapeD...  40.1 us
    unnamed x9, local copies, waits for them, and re-layouts  3.48 us

profile of v1, /device:TPU:11, one launch (start us, length us, event | category | flops | bytes accessed | tf_op | source)
XLA Modules:
  0.0 43.5 jit_solution(4597723907597113741)
XLA Ops:
  0.0 0.0 copy-start.2
  0.0 0.8 %copy.5.members = s32[4,2]{1,0:T(4,128)S(1)} copy(s32[4,2]{0,1:T(2,128)} %param.6) | data formatting | bytes 64 | tf_op args[2]
  0.8 0.0 copy-done.2
  0.8 0.1 copy.6.live_ref
  0.9 0.0 copy-start
  0.9 1.2 %copy-done = bf16[8,8,64,128]{3,2,1,0:T(8,128)(2,1)S(1)} copy-done((bf16[8,8,64,128]{3,2,1,0:T(8,128)(2,1)S(1)}, bf16[8,8,64,128]{3,2,1,0:T(8,128)(2,1)}, u32[]{:S(2)}) %copy-start) | copy-done | bytes 1048600
  2.1 0.0 copy-start.1
  2.1 0.7 %copy-done.1 = bf16[8,8,64]{2,1,0:T(8,128)(2,1)S(1)} copy-done((bf16[8,8,64]{2,1,0:T(8,128)(2,1)S(1)}, bf16[8,8,64]{2,1,0:T(8,128)(2,1)}, u32[]{:S(2)}) %copy-start.1) | copy-done | bytes 8216
  2.8 40.1 %shard_map.46 = f32[384,128]{1,0:T(8,128)S(1)} custom-call(bf16[8,8,64,128]{3,2,1,0:T(8,128)(2,1)S(1)} %copy-done, bf16[8,8,64]{2,1,0:T(8,128)(2,1)S(1)} %copy-done.1, s32[4,2]{1,0:T(4,128)S(1)} %copy.5.members, s32[8,4]{1,0:T(8,128)S(1)} %copy.6.live_ref), custom_call_target="tpu_custom_call" | custom-call | tf_op jit(solution)/shard_map/pallas_call | solution.py:159
  42.9 0.7 %copy.8 = f32[384,128]{1,0:T(8,128)} copy(f32[384,128]{1,0:T(8,128)S(1)} %shard_map.46) | data formatting | bytes 393216
Async XLA Ops:
  0.0 0.8 %copy-start.2 = (s32[8,4]{0,1:T(4,128)S(1)}, s32[8,4]{0,1:T(4,128)}, u32[]{:S(2)}) copy-start(s32[8,4]{0,1:T(4,128)} %param.7) | copy-start | bytes 388
  0.9 1.2 %copy-start = (bf16[8,8,64,128]{3,2,1,0:T(8,128)(2,1)S(1)}, bf16[8,8,64,128]{3,2,1,0:T(8,128)(2,1)}, u32[]{:S(2)}) copy-start(bf16[8,8,64,128]{3,2,1,0:T(8,128)(2,1)} %panels.1) | copy-start | bytes 3145732
  2.1 0.7 %copy-start.1 = (bf16[8,8,64]{2,1,0:T(8,128)(2,1)S(1)}, bf16[8,8,64]{2,1,0:T(8,128)(2,1)}, u32[]{:S(2)}) copy-start(bf16[8,8,64]{2,1,0:T(8,128)(2,1)} %weights.1) | copy-start | bytes 24580

commit v2 on v1

--- a/solution.py
+++ b/solution.py
@@ -15,7 +15,7 @@
     (heldw, root_ref, scaled, acc, gram, arrived,
      psend, precv, wsend, wrecv, gsend, grecv) = scratch[CHUNKS:]
     epochs, rows, params = panels.shape[1:]
-    pairs = members.shape[0]
+    pairs = members.shape[1]
     per_owner = pairs // ntm
     step = epochs // CHUNKS
     s = lax.axis_index("sat")
@@ -84,18 +84,23 @@
         each(nsat, lambda k: panel_copy(c, k).start())
 
     root_ref[...] = jnp.zeros_like(root_ref)
-    live_all = live_ref[...].astype(jnp.float32)
+    root_ref[:pairs, :epochs] = live_ref[...].astype(jnp.float32)
+    live_all = jnp.transpose(root_ref[:128])[:epochs]
     pair_lane = lax.broadcasted_iota(jnp.int32, live_all.shape, 1)
     offsets = [ntm // 2] + [k for k in range(ntm - 1, 0, -1) if k != ntm // 2] + [0]
     slots = [(k, r) for k in offsets for r in range(per_owner)]
     owners = {k: lax.rem(t + k, ntm) for k in offsets}
+
+    row = lax.broadcasted_iota(jnp.int32, (params, params), 0)
+    col = lax.broadcasted_iota(jnp.int32, (params, params), 1)
+    lower, on_diagonal = row >= col, row == col
 
     own_weight.wait()
     each(nsat, lambda k: weight_arrival(k).wait_recv())
     firsts, seconds = [], []
     for n, (k, r) in enumerate(slots):
         pair = owners[k] * per_owner + r
-        first, second = members[pair, 0] // nsat, members[pair, 1] // nsat
+        first, second = members[0, pair] // nsat, members[1, pair] // nsat
         firsts.append(first)
         seconds.append(second)
         u = heldw[first].astype(jnp.float32)
@@ -127,10 +132,11 @@
             if c < CHUNKS - 1:
                 acc[n] = product
                 continue
-            base = r * 3 * params
-            gram[k, base:base + params] = product[:params, :params]
-            gram[k, base + params:base + 2 * params] = -product[:params, params:]
-            gram[k, base + 2 * params:base + 3 * params] = product[params:, params:]
+            second_gram = product[params:, params:]
+            gram[k, r, :params] = jnp.where(lower, product[:params, :params], second_gram)
+            gram[k, r, params:2 * params] = -product[:params, params:]
+            diagonal = jnp.sum(jnp.where(on_diagonal, second_gram, 0.0), axis=0, keepdims=True)
+            gram[k, r, 2 * params:] = jnp.broadcast_to(diagonal, (8, params))
             if k > 0 and r == per_owner - 1:
                 gram_copy(k).start()
 
@@ -138,7 +144,14 @@
     for k in offsets[:-1]:
         gram_copy(k).wait_recv()
         total = total + arrived[k]
-    out_ref[...] = total
+    for r in range(per_owner):
+        base = r * 3 * params
+        packed = total[r, :params]
+        mirrored = jnp.transpose(packed)
+        out_ref[base:base + params] = jnp.where(lower, packed, mirrored)
+        out_ref[base + params:base + 2 * params] = total[r, params:2 * params]
+        second_gram = jnp.where(on_diagonal, total[r, 2 * params:2 * params + 1], mirrored)
+        out_ref[base + 2 * params:base + 3 * params] = jnp.where(row < col, packed, second_gram)
 
     each(nsat, lambda k: weight_copy(k).wait_send())
     for c in range(CHUNKS):
@@ -155,7 +168,7 @@
     root_rows = -(-pairs * epochs // 128) * 128
     dma = pltpu.SemaphoreType.DMA
     vmem = pl.BlockSpec(memory_space=pltpu.VMEM)
-    hbm = pl.BlockSpec(memory_space=pl.ANY)
+    hbm = pl.BlockSpec(memory_space=pltpu.HBM)
     return pl.pallas_call(
         functools.partial(kernel, nsat, ntm),
         out_shape=jax.ShapeDtypeStruct((out_rows, params), jnp.float32),
@@ -167,15 +180,15 @@
             pltpu.VMEM((root_rows, 128), jnp.float32),
             pltpu.VMEM((2, epochs // CHUNKS * rows, 2 * params), jnp.bfloat16),
             pltpu.VMEM((pairs, 2 * params, 2 * params), jnp.float32),
-            pltpu.VMEM((ntm, out_rows, params), jnp.float32),
-            pltpu.VMEM((ntm, out_rows, params), jnp.float32),
+            pltpu.VMEM((ntm, pairs // ntm, 2 * params + 8, params), jnp.float32),
+            pltpu.VMEM((ntm, pairs // ntm, 2 * params + 8, params), jnp.float32),
             dma((CHUNKS, nsat)), dma((CHUNKS, nsat)),
             dma((nsat,)), dma((nsat,)),
             dma((ntm,)), dma((ntm,)),
         ],
         compiler_params=pltpu.CompilerParams(
-            collective_id=0, has_side_effects=True, vmem_limit_bytes=48 << 20),
-    )(panels, weights, pair_members, pair_live)
+            collective_id=0, has_side_effects=True, vmem_limit_bytes=60 << 20),
+    )(panels, weights, pair_members.T, pair_live.T)
 
 
 def solution(mesh):

time: 43.8 us -> 40.3 us (0.920)
  local copies, waits for them, and re-layouts: 3.48 us -> 1.62 us
  Pallas kernels: 40.1 us -> 38.5 us
    unnamed x9 -> x1, local copies, waits for them, and re-layouts: 3.48 us -> 1.62 us
    pallas_call x1, Pallas kernels: 40.1 us -> 38.5 us  [per_device(): pl.pallas_call(functools.partial(kernel, nsat, ntm), out_shape=jax.ShapeD...]
where the time goes in v2:
time: 40.3 us; the launch traced here: 40.1 us
  Pallas kernels  38.5 us (96%)
  local copies, waits for them, and re-layouts  1.62 us (4%)
    pallas_call x1, Pallas kernels, per_device(): pl.pallas_call(functools.partial(kernel, nsat, ntm), out_shape=jax.ShapeD...  38.5 us
    unnamed x1, local copies, waits for them, and re-layouts  1.62 us

profile of v2, /device:TPU:11, one launch (start us, length us, event | category | flops | bytes accessed | tf_op | source)
XLA Modules:
  0.0 40.1 jit_solution(6571713842583633490)
XLA Ops:
  0.0 38.5 %shard_map.46 = f32[384,128]{1,0:T(8,128)} custom-call(bf16[8,8,64,128]{3,2,1,0:T(8,128)(2,1)} %panels.1, bf16[8,8,64]{2,1,0:T(8,128)(2,1)} %weights.1, s32[2,4]{1,0:T(2,128)} %bitcast.3, s32[4,8]{1,0:T(4,128)} %bitcast.2), custom_call_target="tpu_custom_call" | custom-call | tf_op jit(solution)/shard_map/pallas_call | solution.py:172
  38.5 1.6 %copy.6 = f32[384,128]{1,0:T(8,128)} copy(f32[384,128]{1,0:T(8,128)} %shard_map.46) | data formatting | bytes 393216

commit v3 on v2

v3 whole, which is shorter than its diff:
```python
import functools
import jax
import jax.numpy as jnp
from jax import lax
from jax.experimental import pallas as pl
from jax.experimental.pallas import tpu as pltpu
from jax.sharding import PartitionSpec as P

MESH = pl.DeviceIdType.MESH


def chunk_sizes(epochs):
    count = min(epochs, 4)
    return [epochs * (c + 1) // count - epochs * c // count for c in range(count)]


def kernel(nsat, ntm, panels, weights, members, live_ref, out_ref, *scratch):
    epochs, rows, params = panels.shape[1:]
    sizes = chunk_sizes(epochs)
    chunks = range(len(sizes))
    starts = [sum(sizes[:c]) for c in chunks]
    held, scaled, arrived = (scratch[n * len(sizes):(n + 1) * len(sizes)] for n in range(3))
    heldw, root_ref, psend, precv, wsend, wrecv, fsend, frecv = scratch[3 * len(sizes):]
    pairs = members.shape[1]
    per_owner = pairs // ntm
    s = lax.axis_index("sat")
    t = lax.axis_index("tm")

    barrier = pltpu.get_barrier_semaphore()

    def greet(axis, me, n):
        def body(k, carry):
            pl.semaphore_signal(barrier, inc=1, device_id={axis: lax.rem(me + k, n)}, device_id_type=MESH)
            return carry
        lax.fori_loop(1, n, body, 0)

    greet("sat", s, nsat)
    greet("tm", t, ntm)

    def weight_copy(k):
        dest = lax.rem(s + k, nsat)
        return pltpu.make_async_remote_copy(
            src_ref=weights.at[dest], dst_ref=heldw.at[s],
            send_sem=wsend.at[k], recv_sem=wrecv.at[k],
            device_id={"sat": dest}, device_id_type=MESH)

    def weight_arrival(k):
        source = lax.rem(s + nsat - k, nsat)
        return pltpu.make_async_remote_copy(
            src_ref=weights.at[s], dst_ref=heldw.at[source],
            send_sem=wsend.at[k], recv_sem=wrecv.at[k],
            device_id={"sat": source}, device_id_type=MESH)

    def panel_copy(c, k):
        dest = lax.rem(s + k, nsat)
        part = pl.ds(starts[c], sizes[c])
        return pltpu.make_async_remote_copy(
            src_ref=panels.at[dest, part], dst_ref=held[c].at[s],
            send_sem=psend.at[c, k], recv_sem=precv.at[c, k],
            device_id={"sat": dest}, device_id_type=MESH)

    def panel_arrival(c, k):
        source = lax.rem(s + nsat - k, nsat)
        part = pl.ds(starts[c], sizes[c])
        return pltpu.make_async_remote_copy(
            src_ref=panels.at[s, part], dst_ref=held[c].at[source],
            send_sem=psend.at[c, k], recv_sem=precv.at[c, k],
            device_id={"sat": source}, device_id_type=MESH)

    own_panels = [
        pltpu.make_async_copy(panels.at[s, pl.ds(starts[c], sizes[c])], held[c].at[s], psend.at[c, 0])
        for c in chunks
    ]
    own_weight = pltpu.make_async_copy(weights.at[s], heldw.at[s], wsend.at[0])
    for copy in own_panels:
        copy.start()
    own_weight.start()

    pl.semaphore_wait(barrier, nsat - 1 + ntm - 1)

    def each(n, f):
        def body(k, carry):
            f(k)
            return carry
        lax.fori_loop(1, n, body, 0)

    each(nsat, lambda k: weight_copy(k).start())
    for c in chunks:
        each(nsat, lambda k: panel_copy(c, k).start())

    root_ref[...] = jnp.zeros_like(root_ref)
    root_ref[:pairs, :epochs] = live_ref[...].astype(jnp.float32)
    live_all = jnp.transpose(root_ref[:128])[:epochs]
    pair_lane = lax.broadcasted_iota(jnp.int32, live_all.shape, 1)
    offsets = [ntm // 2] + [k for k in range(ntm - 1, 0, -1) if k != ntm // 2] + [0]
    slots = [(k, r) for k in offsets for r in range(per_owner)]
    owners = {k: lax.rem(t + k, ntm) for k in offsets}

    own_weight.wait()
    each(nsat, lambda k: weight_arrival(k).wait_recv())
    firsts, seconds = [], []
    for n, (k, r) in enumerate(slots):
        pair = owners[k] * per_owner + r
        first, second = members[0, pair] // nsat, members[1, pair] // nsat
        firsts.append(first)
        seconds.append(second)
        u = heldw[first].astype(jnp.float32)
        v = heldw[second].astype(jnp.float32)
        live = jnp.sum(jnp.where(pair_lane == pair, live_all, 0.0), axis=1, keepdims=True)
        root_ref[n * epochs:(n + 1) * epochs, :rows] = jnp.sqrt(live * u * v / (u + v))
    root = jnp.transpose(root_ref[...])

    def forward(c, k):
        return pltpu.make_async_remote_copy(
            src_ref=scaled[c].at[k], dst_ref=arrived[c].at[k],
            send_sem=fsend.at[c, k], recv_sem=frecv.at[c, k],
            device_id={"tm": lax.rem(t + k, ntm)}, device_id_type=MESH)

    totals = [jnp.zeros((2 * params, 2 * params), jnp.float32)] * per_owner

    def add_rows(block):
        for r in range(per_owner):
            both = block[r]
            totals[r] += lax.dot_general(both, both, (((0,), (0,)), ((), ())), preferred_element_type=jnp.float32)

    def add_arrived(c):
        for k in reversed(offsets[:-1]):
            forward(c, k).wait_recv()
            add_rows(arrived[c].at[k])

    for c in chunks:
        own_panels[c].wait()
        each(nsat, lambda k: panel_arrival(c, k).wait_recv())
        for n, (k, r) in enumerate(slots):
            for e in range(sizes[c]):
                at = n * epochs + starts[c] + e
                column = root[:rows, at:at + 1]
                here = slice(e * rows, (e + 1) * rows)
                scaled[c][k, r, here, :params] = (column * held[c][firsts[n], e].astype(jnp.float32)).astype(jnp.bfloat16)
                scaled[c][k, r, here, params:] = (column * held[c][seconds[n], e].astype(jnp.float32)).astype(jnp.bfloat16)
            if k > 0 and r == per_owner - 1:
                forward(c, k).start()
        add_rows(scaled[c].at[0])
    for c in chunks:
        add_arrived(c)

    for r in range(per_owner):
        base = r * 3 * params
        out_ref[base:base + params] = totals[r][:params, :params]
        out_ref[base + params:base + 2 * params] = -totals[r][:params, params:]
        out_ref[base + 2 * params:base + 3 * params] = totals[r][params:, params:]

    each(nsat, lambda k: weight_copy(k).wait_send())
    for c in chunks:
        each(nsat, lambda k: panel_copy(c, k).wait_send())
        for k in offsets[:-1]:
            forward(c, k).wait_send()


def per_device(panels, weights, pair_members, pair_live):
    nsat, ntm = lax.axis_size("sat"), lax.axis_size("tm")
    sats, epochs, rows, params = panels.shape
    pairs = pair_members.shape[0]
    sizes = chunk_sizes(epochs)
    out_rows = pairs // ntm * 3 * params
    root_rows = -(-pairs * epochs // 128) * 128
    dma = pltpu.SemaphoreType.DMA
    vmem = pl.BlockSpec(memory_space=pltpu.VMEM)
    hbm = pl.BlockSpec(memory_space=pltpu.HBM)
    return pl.pallas_call(
        functools.partial(kernel, nsat, ntm),
        out_shape=jax.ShapeDtypeStruct((out_rows, params), jnp.float32),
        in_specs=[hbm, hbm, pl.BlockSpec(memory_space=pltpu.SMEM), vmem],
        out_specs=vmem,
        scratch_shapes=[
            *[pltpu.VMEM((nsat, size, rows, params), jnp.bfloat16) for size in sizes],
            *[pltpu.VMEM((ntm, pairs // ntm, size * rows, 2 * params), jnp.bfloat16) for size in sizes] * 2,
            pltpu.VMEM((nsat, epochs, rows), jnp.bfloat16),
            pltpu.VMEM((root_rows, 128), jnp.float32),
            dma((len(sizes), nsat)), dma((len(sizes), nsat)),
            dma((nsat,)), dma((nsat,)),
            dma((len(sizes), ntm)), dma((len(sizes), ntm)),
        ],
        compiler_params=pltpu.CompilerParams(
            collective_id=0, has_side_effects=True, vmem_limit_bytes=60 << 20),
    )(panels, weights, pair_members.T, pair_live.T)


def solution(mesh):
    in_specs = (P("sat", "tm", None, None), P("sat", "tm", None), P("sat", None), P("tm", "sat"))
    out_specs = P(("sat", "tm"), None)
    return jax.shard_map(
        per_device, mesh=mesh, in_specs=in_specs, out_specs=out_specs, check_vma=False
    )
```

time: 40.3 us -> 37.6 us (0.933)
  Pallas kernels: 38.5 us -> 35.7 us
    pallas_call x1, Pallas kernels: 38.5 us -> 35.7 us  [per_device(): pl.pallas_call(functools.partial(kernel, nsat, ntm), out_shape=jax.ShapeD...]
where the time goes in v3:
time: 37.6 us; the launch traced here: 37.4 us
  Pallas kernels  35.7 us (95%)
  local copies, waits for them, and re-layouts  1.62 us (4%)
    pallas_call x1, Pallas kernels, per_device(): pl.pallas_call(functools.partial(kernel, nsat, ntm), out_shape=jax.ShapeD...  35.7 us
    unnamed x1, local copies, waits for them, and re-layouts  1.62 us

profile of v3, /device:TPU:11, one launch (start us, length us, event | category | flops | bytes accessed | tf_op | source)
XLA Modules:
  0.0 37.4 jit_solution(292796790196568600)
XLA Ops:
  0.0 35.7 %shard_map.46 = f32[384,128]{1,0:T(8,128)} custom-call(bf16[8,8,64,128]{3,2,1,0:T(8,128)(2,1)} %panels.1, bf16[8,8,64]{2,1,0:T(8,128)(2,1)} %weights.1, s32[2,4]{1,0:T(2,128)} %bitcast.3, s32[4,8]{1,0:T(4,128)} %bitcast.2), custom_call_target="tpu_custom_call" | custom-call | tf_op jit(solution)/shard_map/pallas_call | solution.py:170
  35.8 1.6 %copy.6 = f32[384,128]{1,0:T(8,128)} copy(f32[384,128]{1,0:T(8,128)} %shard_map.46) | data formatting | bytes 393216

commit v4 on v3

--- a/solution.py
+++ b/solution.py
@@ -12,6 +12,14 @@
 def chunk_sizes(epochs):
     count = min(epochs, 4)
     return [epochs * (c + 1) // count - epochs * c // count for c in range(count)]
+
+
+def partner(me, k, n):
+    place, other = 1, 0
+    while place < n:
+        other = other + lax.rem(me // place + k // place, 2) * place
+        place *= 2
+    return other
 
 
 def kernel(nsat, ntm, panels, weights, members, live_ref, out_ref, *scratch):
@@ -32,7 +40,7 @@
         def body(k, carry):
             pl.semaphore_signal(barrier, inc=1, device_id={axis: lax.rem(me + k, n)}, device_id_type=MESH)
             return carry
-        lax.fori_loop(1, n, body, 0)
+        lax.fori_loop(1, n, body, 0, unroll=True)
 
     greet("sat", s, nsat)
     greet("tm", t, ntm)
@@ -82,19 +90,20 @@
         def body(k, carry):
             f(k)
             return carry
-        lax.fori_loop(1, n, body, 0)
-
-    each(nsat, lambda k: weight_copy(k).start())
+        lax.fori_loop(1, n, body, 0, unroll=True)
+
     for c in chunks:
         each(nsat, lambda k: panel_copy(c, k).start())
+        if c == 0:
+            each(nsat, lambda k: weight_copy(k).start())
 
     root_ref[...] = jnp.zeros_like(root_ref)
     root_ref[:pairs, :epochs] = live_ref[...].astype(jnp.float32)
     live_all = jnp.transpose(root_ref[:128])[:epochs]
     pair_lane = lax.broadcasted_iota(jnp.int32, live_all.shape, 1)
-    offsets = [ntm // 2] + [k for k in range(ntm - 1, 0, -1) if k != ntm // 2] + [0]
+    offsets = list(range(2, ntm)) + [1, 0]
     slots = [(k, r) for k in offsets for r in range(per_owner)]
-    owners = {k: lax.rem(t + k, ntm) for k in offsets}
+    owners = {k: partner(t, k, ntm) for k in offsets}
 
     own_weight.wait()
     each(nsat, lambda k: weight_arrival(k).wait_recv())
@@ -114,7 +123,7 @@
         return pltpu.make_async_remote_copy(
             src_ref=scaled[c].at[k], dst_ref=arrived[c].at[k],
             send_sem=fsend.at[c, k], recv_sem=frecv.at[c, k],
-            device_id={"tm": lax.rem(t + k, ntm)}, device_id_type=MESH)
+            device_id={"tm": owners[k]}, device_id_type=MESH)
 
     totals = [jnp.zeros((2 * params, 2 * params), jnp.float32)] * per_owner
 

time: 37.6 us -> 37.4 us (level)
  no operation moved by 1% of the time
where the time goes in v4:
time: 37.4 us; the launch traced here: 37.2 us
  Pallas kernels  35.6 us (95%)
  local copies, waits for them, and re-layouts  1.62 us (4%)
    pallas_call x1, Pallas kernels, per_device(): pl.pallas_call(functools.partial(kernel, nsat, ntm), out_shape=jax.ShapeD...  35.6 us
    unnamed x1, local copies, waits for them, and re-layouts  1.62 us

profile of v4, /device:TPU:11, one launch (start us, length us, event | category | flops | bytes accessed | tf_op | source)
XLA Modules:
  0.0 37.2 jit_solution(15948349782165751842)
XLA Ops:
  0.0 35.6 %shard_map.46 = f32[384,128]{1,0:T(8,128)} custom-call(bf16[8,8,64,128]{3,2,1,0:T(8,128)(2,1)} %panels.1, bf16[8,8,64]{2,1,0:T(8,128)(2,1)} %weights.1, s32[2,4]{1,0:T(2,128)} %bitcast.3, s32[4,8]{1,0:T(4,128)} %bitcast.2), custom_call_target="tpu_custom_call" | custom-call | tf_op jit(solution)/shard_map/pallas_call | solution.py:179
  35.6 1.6 %copy.6 = f32[384,128]{1,0:T(8,128)} copy(f32[384,128]{1,0:T(8,128)} %shard_map.46) | data formatting | bytes 393216
